TPU v7x, 32 devices: a whole 2x2x4 slice. The times are simulated.
32 devices in a mesh: band: 16 (over z, y, x), mem: 2 (over core).
Axes of the slice: x: 2, y: 2, z: 4, core: 2. Of those that a mesh axis runs over, the one named last changes fastest.
Arguments:
- state: float32 [16384, 2048], P('band', 'mem'), may hold values from -10 to 10
- obs_anom: bfloat16 [4096, 2048], P('band', 'mem'), may hold values from -8 to 8
- innov: float32 [4096, 2048], P('band', 'mem'), may hold values from -12 to 12
- pattern: int32 [16, 4, 8, 4], P('band'), may hold values 0 or 1
- distance: int32 [16, 4, 8, 4], P('band'), may hold values from 0 to 7
- taper: float32 [8], replicated, may hold values from 0.2 to 1
- order: int32 [16, 4], P('band'), may hold values from 0 to 3, each once within a row
Outputs:
- analysis: float32 [16384, 2048], P('band', 'mem')
Inputs may be any that keep to these rules, and one draw needn't show every extreme that they name: Each row of order lists 0 .. 3 once each.
All inputs are finite; a program needn't handle non-finite values. No bound on the sum of `pattern` on one device may be relied on, other than what follows from the above.
Results may differ from a plain program's by a relative error of at most 0.0028.
Values may be sent and summed in bfloat16 or wider, within the bound.
A program may use at most 64 MiB of HBM per device.

v0:
```python
import jax
import jax.numpy as jnp
from jax import lax
from jax.sharding import PartitionSpec as P


def from_behind(value, axis, steps):
    count = lax.axis_size(axis)
    pairs = [(source, (source + steps) % count) for source in range(count)]
    return lax.ppermute(value, axis, pairs)


def spread(blocks):
    rows, cols = blocks.shape
    return jnp.broadcast_to(blocks[:, None, :, None], (rows, 128, cols, 64)).reshape(
        rows * 128, cols * 64
    )


def on_device(state, obs_anom, innov, pattern, distance, taper, order):
    members = lax.axis_size("mem") * state.shape[1]
    scale = 1.0 / (members - 1)
    num_obs = obs_anom.shape[0]
    arrivals = order.shape[1]
    gram_part = jnp.dot(obs_anom, obs_anom.T, preferred_element_type=jnp.float32)
    gram = lax.psum(gram_part, "mem")
    spd = gram * scale + jnp.eye(num_obs, dtype=jnp.float32)
    factor = jnp.linalg.cholesky(spd)
    weights_own = jax.scipy.linalg.cho_solve((factor, True), innov).astype(jnp.bfloat16)
    own_batch = jnp.stack([obs_anom, weights_own])
    batches = [own_batch]
    current = own_batch
    for offset in range(1, arrivals):
        current = from_behind(current, "band", 1)
        batches.append(current)
    stacked = jnp.stack(batches)
    onehot = (distance[0][..., None] == jnp.arange(taper.shape[0], dtype=jnp.int32)).astype(
        jnp.float32
    )
    local = pattern[0].astype(jnp.float32) * jnp.sum(onehot * taper, axis=-1)
    field = state
    for step in range(arrivals):
        offset = order[0, step]
        chosen = lax.dynamic_index_in_dim(stacked, offset, 0, keepdims=False)
        y_batch = chosen[0].astype(jnp.float32)
        w_batch = chosen[1].astype(jnp.float32)
        blocks = lax.dynamic_index_in_dim(local, offset, 0, keepdims=False)
        cross_part = jnp.dot(field, y_batch.T, precision=lax.Precision.HIGHEST)
        cross = lax.psum(cross_part, "mem")
        field = field + jnp.dot(
            cross * scale * spread(blocks), w_batch, precision=lax.Precision.HIGHEST
        )
    return field


def solution(mesh):
    return jax.shard_map(
        on_device,
        mesh=mesh,
        in_specs=(
            P("band", "mem"),
            P("band", "mem"),
            P("band", "mem"),
            P("band", None, None, None),
            P("band", None, None, None),
            P(),
            P("band", None),
        ),
        out_specs=P("band", "mem"),
        check_vma=False,
    )
```

profile of v0, /device:TPU:0, one launch (start us, length us, event | category | flops | bytes accessed | tf_op | source)
XLA Modules:
  0.0 313.7 jit_solution(5123660919342085485)
XLA Ops:
  6.5 2.3 fusion.45
  8.9 0.0 all-reduce.7.cloned.1.call-update
  8.9 0.0 all-reduce.9.cloned.1.call-start
  9.0 21.7 %all-reduce.7.cloned.1.call-done = f32[256,256]{0,1:T(8,128)} async-done(((f32[256,256]{0,1:T(8,128)}), f32[256,256]{0,1:T(8,128)}) %all-reduce.7.cloned.1.call-update) | async-done | bytes 262160 | tf_op jit(solution)/shard_map/psum | solution.py:26
  30.6 1.0 convert_add_fusion
  31.6 0.1 copy.12
  31.8 1.0 fusion.18
  32.8 11.7 %cholesky.50 = f32[128,128]{1,0:T(8,128)S(1)} custom-call(f32[128,128]{1,0:T(8,128)S(1)} %cholesky.118), custom_call_target="Cholesky" | custom-call | tf_op jit(solution)/shard_map/jit(cholesky)/cholesky | solution.py:28
  44.5 9.8 %custom-call.18 = f32[1,128,128]{1,2,0:T(8,128)S(1)} custom-call(f32[1,128,128]{2,1,0:T(8,128)S(1)} %get-tuple-element.28), custom_call_target="InvertDiagBlocksLowerTriangular" | custom-call | tf_op jit(solution)/shard_map/jit(cholesky)/cholesky | solution.py:28
  54.4 0.2 constant_dynamic-update-slice_fusion
  54.6 0.3 convolution_subtract_fusion.2
  54.9 11.7 %cholesky.105 = f32[128,128]{1,0:T(8,128)S(1)} custom-call(f32[128,128]{1,0:T(8,128)S(1)} %convolution_subtract_fusion.2), custom_call_target="Cholesky" | custom-call | tf_op jit(solution)/shard_map/jit(cholesky)/cholesky | solution.py:28
  66.6 0.7 compare_reduce_fusion
  68.7 0.1 triangular_solve.73
  68.8 4.2 %while.1 = (s32[]{:T(128)}, f32[256,256]{1,0:T(8,128)S(1)}, s32[2,2]{1,0:T(2,128)S(1)}, f32[2,128,128]{2,1,0:T(8,128)S(1)}, s32[]{:T(128)}) while((s32[]{:T(128)}, f32[256,256]{1,0:T(8,128)S(1)}, s32[2,2]{1,0:T(2,128)S(1)}, f32[2,128,128]{2,1,0:T(8,128)S(1)}, s32[]{:T(128)}) %tuple.30), condition=%wide.while_cond, body=%wide.while_body.sunk | while | flops 2 | bytes 131181 | solution.py:29
  68.9 0.6 fusion.60
  69.5 1.4 bitcast_dynamic-update-slice_fusion.2
  70.9 0.6 fusion.60
  71.5 1.4 bitcast_dynamic-update-slice_fusion.2
  73.0 0.0 copy-start.5
  73.0 19.7 %custom-call.19 = f32[2,128,128]{1,2,0:T(8,128)S(1)} custom-call(f32[2,128,128]{2,1,0:T(8,128)S(1)} %get-tuple-element.12), custom_call_target="InvertDiagBlocksLowerTriangular" | custom-call | tf_op jit(solution)/shard_map/jit(_cho_solve)/triangular_solve | solution.py:29
  92.7 0.6 fusion.16
  93.3 0.6 convolution_subtract_fusion.1
  93.9 0.0 copy-start.9
  93.9 0.6 fusion.23
  94.5 0.6 fusion.22
  95.1 0.6 convolution_subtract_fusion
  95.8 0.6 fusion
  96.4 0.2 fusion.42
  96.6 1.8 collective-permute-start
  98.4 27.3 %collective-permute-done = bf16[2,256,1024]{2,1,0:T(8,128)(2,1)S(1)} collective-permute-done((bf16[2,256,1024]{2,1,0:T(8,128)(2,1)S(1)}, bf16[2,256,1024]{2,1,0:T(8,128)(2,1)S(1)}, u32[]{:S(2)}, u32[]{:S(2)}) %collective-permute-start) | collective-permute-done | bytes 1048608 | tf_op jit(solution)/shard_map/ppermute | solution.py:10
  125.7 28.3 %collective-permute-done.1 = bf16[2,256,1024]{2,1,0:T(8,128)(2,1)} collective-permute-done((bf16[2,256,1024]{2,1,0:T(8,128)(2,1)S(1)}, bf16[2,256,1024]{2,1,0:T(8,128)(2,1)}, u32[]{:S(2)}, u32[]{:S(2)}) %collective-permute-start.1) | collective-permute-done | bytes 1048608 | tf_op jit(solution)/shard_map/ppermute | solution.py:10
  153.9 0.7 fusion.44
  156.6 25.0 %collective-permute-done.2 = bf16[2,256,1024]{2,1,0:T(8,128)(2,1)} collective-permute-done((bf16[2,256,1024]{2,1,0:T(8,128)(2,1)}, bf16[2,256,1024]{2,1,0:T(8,128)(2,1)}, u32[]{:S(2)}, u32[]{:S(2)}) %collective-permute-start.2) | collective-permute-done | bytes 1048608 | tf_op jit(solution)/shard_map/ppermute | solution.py:10
  181.6 1.9 pad_maximum_fusion
  183.5 1.9 copy-done.3
  185.5 3.2 %convolution_bitcast_fusion = f32[1024,256]{0,1:T(8,128)} fusion(f32[1024,1024]{1,0:T(8,128)S(1)} %copy-done.4, bf16[4,2,256,1024]{3,2,1,0:T(8,128)(2,1)S(1)} %pad_maximum_fusion, s32[]{:T(128)S(6)} %select_n.23), kind=kOutput, calls=%fused_computation.7 | convolution fusion | flops 3221225472 | bytes 5767172 | tf_op jit(solution)/shard_map/dot_general | solution.py:48
  188.6 0.0 all-reduce.9.cloned.1.call-update
  188.6 0.3 all-reduce.11.cloned.1.call-start
  194.7 0.2 select_reduce_fusion
  195.0 9.1 %all-reduce.9.cloned.1.call-done = f32[1024,256]{0,1:T(8,128)} async-done(((f32[1024,256]{0,1:T(8,128)}), f32[1024,256]{0,1:T(8,128)}) %all-reduce.9.cloned.1.call-update) | async-done | bytes 1048592 | tf_op jit(solution)/shard_map/psum | solution.py:49
  204.1 0.1 broadcast_in_dim.19
  204.2 4.9 %convolution_add_fusion.3 = f32[1024,1024]{1,0:T(8,128)S(1)} fusion(f32[1024,1024]{1,0:T(8,128)} %param.7, f32[32,8,8,128]{3,2,1,0:T(8,128)S(1)} %bitcast.125, f32[1024,256]{0,1:T(8,128)} %all-reduce.9.cloned.1.call-done, bf16[4,2,256,1024]{3,2,1,0:T(8,128)(2,1)} %copy-done.3, s32[]{:T(128)S(6)} %select_n.23, s32[]{:T(128)S(6)} %add.80), kind=kOutput, calls=%fused_computation.6 | convolution fusion | flops 3222798336 | bytes 11010056 | tf_op jit(solution)/shard_map/dot_general | solution.py:50
  209.1 0.0 copy-start.2
  209.1 2.0 copy-done.2
  211.1 4.2 %fusion.11 = f32[1024,256]{0,1:T(8,128)} fusion(f32[1024,1024]{1,0:T(8,128)S(1)} %convolution_add_fusion.3, bf16[4,2,256,1024]{3,2,1,0:T(8,128)(2,1)} %copy-done.3, s32[]{:T(128)S(6)} %select_n.24), kind=kOutput, calls=%fused_computation.34 | convolution fusion | flops 3221225472 | bytes 5767172 | tf_op jit(solution)/shard_map/dot_general | solution.py:48
  215.4 0.0 all-reduce.11.cloned.1.call-update
  215.4 0.0 all-reduce.13.cloned.1.call-start
  215.5 20.7 %all-reduce.11.cloned.1.call-done = f32[1024,256]{0,1:T(8,128)} async-done(((f32[1024,256]{0,1:T(8,128)}), f32[1024,256]{0,1:T(8,128)}) %all-reduce.11.cloned.1.call-update) | async-done | bytes 1048592 | tf_op jit(solution)/shard_map/psum | solution.py:49
  236.2 0.1 broadcast_in_dim.39
  236.3 4.9 %convolution_add_fusion.2 = f32[1024,1024]{1,0:T(8,128)S(1)} fusion(f32[1024,1024]{1,0:T(8,128)} %copy-done.2, f32[32,8,8,128]{3,2,1,0:T(8,128)S(1)} %bitcast.123, f32[1024,256]{0,1:T(8,128)} %all-reduce.11.cloned.1.call-done, bf16[4,2,256,1024]{3,2,1,0:T(8,128)(2,1)} %copy-done.3, s32[]{:T(128)S(6)} %select_n.24, s32[]{:T(128)S(6)} %add.80), kind=kOutput, calls=%fused_computation.5 | convolution fusion | flops 3222798336 | bytes 11010056 | tf_op jit(solution)/shard_map/dot_general | solution.py:50
  241.2 2.0 copy-done.1
  243.2 4.2 %fusion.10 = f32[1024,256]{0,1:T(8,128)} fusion(f32[1024,1024]{1,0:T(8,128)S(1)} %convolution_add_fusion.2, bf16[4,2,256,1024]{3,2,1,0:T(8,128)(2,1)} %copy-done.3, s32[]{:T(128)S(6)} %select_n.25), kind=kOutput, calls=%fused_computation.31 | convolution fusion | flops 3221225472 | bytes 5767172 | tf_op jit(solution)/shard_map/dot_general | solution.py:48
  247.5 0.0 all-reduce.13.cloned.1.call-update
  247.5 0.3 all-reduce.15.cloned.1.call-start
  247.8 20.5 %all-reduce.13.cloned.1.call-done = f32[1024,256]{0,1:T(8,128)} async-done(((f32[1024,256]{0,1:T(8,128)}), f32[1024,256]{0,1:T(8,128)}) %all-reduce.13.cloned.1.call-update) | async-done | bytes 1048592 | tf_op jit(solution)/shard_map/psum | solution.py:49
  268.3 0.1 broadcast_in_dim.41
  268.4 4.9 %convolution_add_fusion.1 = f32[1024,1024]{1,0:T(8,128)S(1)} fusion(f32[1024,1024]{1,0:T(8,128)} %copy-done.1, f32[32,8,8,128]{3,2,1,0:T(8,128)S(1)} %bitcast.124, f32[1024,256]{0,1:T(8,128)} %all-reduce.13.cloned.1.call-done, bf16[4,2,256,1024]{3,2,1,0:T(8,128)(2,1)} %copy-done.3, s32[]{:T(128)S(6)} %select_n.25, s32[]{:T(128)S(6)} %add.80), kind=kOutput, calls=%fused_computation.4 | convolution fusion | flops 3222798336 | bytes 11010056 | tf_op jit(solution)/shard_map/dot_general | solution.py:50
  273.3 2.0 copy-done
  275.3 4.3 %fusion.9 = f32[1024,256]{0,1:T(8,128)} fusion(f32[1024,1024]{1,0:T(8,128)S(1)} %convolution_add_fusion.1, bf16[4,2,256,1024]{3,2,1,0:T(8,128)(2,1)} %copy-done.3, s32[]{:T(128)S(6)} %select_n.26), kind=kOutput, calls=%fused_computation.28 | convolution fusion | flops 3221225472 | bytes 5767172 | tf_op jit(solution)/shard_map/dot_general | solution.py:48
  279.6 0.0 all-reduce.15.cloned.1.call-update
  279.6 20.8 %all-reduce.15.cloned.1.call-done = f32[1024,256]{0,1:T(8,128)} async-done(((f32[1024,256]{0,1:T(8,128)}), f32[1024,256]{0,1:T(8,128)}) %all-reduce.15.cloned.1.call-update) | async-done | bytes 1048592 | tf_op jit(solution)/shard_map/psum | solution.py:49
  300.3 0.1 broadcast_in_dim.43
  300.5 6.7 %convolution_add_fusion = f32[1024,1024]{1,0:T(8,128)} fusion(f32[1024,1024]{1,0:T(8,128)} %copy-done, f32[32,8,8,128]{3,2,1,0:T(8,128)S(1)} %bitcast.122, f32[1024,256]{0,1:T(8,128)} %all-reduce.15.cloned.1.call-done, bf16[4,2,256,1024]{3,2,1,0:T(8,128)(2,1)} %copy-done.3, s32[]{:T(128)S(6)} %select_n.26, s32[]{:T(128)S(6)} %add.80), kind=kOutput, calls=%fused_computation.3 | convolution fusion | flops 3222798336 | bytes 11010056 | tf_op jit(solution)/shard_map/dot_general | solution.py:50
  (30 shorter events, 0.2 us)
Async XLA Ops:
  6.5 86.1 %copy-start.6 = (f32[256,1024]{1,0:T(8,128)S(1)}, f32[256,1024]{1,0:T(8,128)}, u32[]{:S(2)}) copy-start(f32[256,1024]{1,0:T(8,128)} %param.9) | copy-start | bytes 3145732
  6.5 24.1 %all-reduce.7.cloned.1.call-start = ((), (), s32[]{:S(2)}) async-start(), calls=%async_computation | async-start | bytes 524288 | tf_op jit(solution)/shard_map/psum | solution.py:26
  8.9 195.2 %all-reduce.9.cloned.1.call-start = ((), (), s32[]{:S(2)}) async-start(), calls=%async_computation.1 | async-start | bytes 2097152 | tf_op jit(solution)/shard_map/psum | solution.py:49
  73.0 23.4 %copy-start.5 = (bf16[256,1024]{1,0:T(8,128)(2,1)S(1)}, bf16[256,1024]{1,0:T(8,128)(2,1)}, u32[]{:S(2)}) copy-start(bf16[256,1024]{1,0:T(8,128)(2,1)} %param.8) | copy-start | bytes 1572868
  93.9 60.0 %copy-start.9 = (s32[1,4]{1,0:T(1,128)S(1)}, s32[1,4]{1,0:T(1,128)}, u32[]{:S(2)}) copy-start(s32[1,4]{1,0:T(1,128)} %param.13) | copy-start | bytes 52
  96.6 29.1 %collective-permute-start = (bf16[2,256,1024]{2,1,0:T(8,128)(2,1)S(1)}, bf16[2,256,1024]{2,1,0:T(8,128)(2,1)S(1)}, u32[]{:S(2)}, u32[]{:S(2)}) collective-permute-start(bf16[2,256,1024]{2,1,0:T(8,128)(2,1)S(1)} %get-tuple-element.24), channel_id=1, source_target_pairs={{0,2},{2,4},{4,6},{6,8},{8,10},{10,12},{12,14},{14,16},{16,18},{18... | collective-permute-start | bytes 3145736 | tf_op jit(solution)/shard_map/ppermute | solution.py:10
  125.7 28.3 %collective-permute-start.1 = (bf16[2,256,1024]{2,1,0:T(8,128)(2,1)S(1)}, bf16[2,256,1024]{2,1,0:T(8,128)(2,1)}, u32[]{:S(2)}, u32[]{:S(2)}) collective-permute-start(bf16[2,256,1024]{2,1,0:T(8,128)(2,1)S(1)} %collective-permute-done), channel_id=1, source_target_pairs={{0,2},{2,4},{4,6},{6,8},{8,10},{10,12},{12,14},{14,16},{16,18},{18... | collective-permute-start | bytes 3145736 | tf_op jit(solution)/shard_map/ppermute | solution.py:10
  153.9 27.6 %collective-permute-start.2 = (bf16[2,256,1024]{2,1,0:T(8,128)(2,1)}, bf16[2,256,1024]{2,1,0:T(8,128)(2,1)}, u32[]{:S(2)}, u32[]{:S(2)}) collective-permute-start(bf16[2,256,1024]{2,1,0:T(8,128)(2,1)} %collective-permute-done.1), channel_id=1, source_target_pairs={{0,2},{2,4},{4,6},{6,8},{8,10},{10,12},{12,14},{14,16},{16,18},{18... | collective-permute-start | bytes 3145736 | tf_op jit(solution)/shard_map/ppermute | solution.py:10
  181.6 3.9 %copy-start.4 = (f32[1024,1024]{1,0:T(8,128)S(1)}, f32[1024,1024]{1,0:T(8,128)}, u32[]{:S(2)}) copy-start(f32[1024,1024]{1,0:T(8,128)} %param.7) | copy-start | bytes 12582916
  183.5 1.9 copy-start.3
  185.4 9.3 %copy-start.8 = (s32[1,4,8,4]{2,3,1,0:T(4,128)S(1)}, s32[1,4,8,4]{2,3,1,0:T(4,128)}, u32[]{:S(2)}) copy-start(s32[1,4,8,4]{2,3,1,0:T(4,128)} %param.11) | copy-start | bytes 1540
  185.4 9.3 %copy-start.10 = (f32[8]{0:T(128)S(1)}, f32[8]{0:T(128)}, u32[]{:S(2)}) copy-start(f32[8]{0:T(128)} %param.12) | copy-start | bytes 100
  185.5 9.5 %copy-start.7 = (s32[1,4,8,4]{2,3,1,0:T(4,128)S(1)}, s32[1,4,8,4]{2,3,1,0:T(4,128)}, u32[]{:S(2)}) copy-start(s32[1,4,8,4]{2,3,1,0:T(4,128)} %param.10) | copy-start | bytes 1540
  188.6 47.5 %all-reduce.11.cloned.1.call-start = ((), (), s32[]{:S(2)}) async-start(), calls=%async_computation.2 | async-start | bytes 2097152 | tf_op jit(solution)/shard_map/psum | solution.py:49
  209.1 2.0 copy-start.2
  215.4 52.9 %all-reduce.13.cloned.1.call-start = ((), (), s32[]{:S(2)}) async-start(), calls=%async_computation.3 | async-start | bytes 2097152 | tf_op jit(solution)/shard_map/psum | solution.py:49
  241.2 2.0 copy-start.1
  247.5 52.9 %all-reduce.15.cloned.1.call-start = ((), (), s32[]{:S(2)}) async-start(), calls=%async_computation.4 | async-start | bytes 2097152 | tf_op jit(solution)/shard_map/psum | solution.py:49
  273.3 2.0 copy-start
Sparse Core Ops, SparseCore 0:
  9.7 20.9 all-reduce.6
  188.8 15.2 all-reduce.8
  215.5 20.5 all-reduce.10
  247.6 20.6 all-reduce.12
  279.7 20.5 all-reduce.14
where the time goes:
time: 314 us
  waiting for transfers between devices  173 us (55%)
  other arithmetic  58 us (18%)
  matrix products  43.7 us (14%)
  between operations  22.5 us (7%)
  local copies, waits for them, and re-layouts  13.5 us (4%)
    ppermute x3, waiting for transfers between devices, from_behind(): return lax.ppermute(value, axis, pairs)  80.5 us
    psum x4, waiting for transfers between devices, on_device(): cross = lax.psum(cross_part, 'mem')  71 us
    another operation x6, other arithmetic, on_device(): factor = jnp.linalg.cholesky(spd)  34 us
    psum x1, waiting for transfers between devices, on_device(): gram = lax.psum(gram_part, 'mem')  21.7 us
    dot_general x4, matrix products, on_device(): jnp.dot(cross * scale * spread(blocks), w_batch, precision=lax.Precision....  21.4 us
    another operation x4, other arithmetic, on_device(): jax.scipy.linalg.cho_solve((factor, True), innov).astype(jnp.bfloat16)  19.7 us
    dot_general x4, matrix products, on_device(): cross_part = jnp.dot(field, y_batch.T, precision=lax.Precision.HIGHEST)  15.9 us
    unnamed x22, local copies, waits for them, and re-layouts  7.98 us
  transfers between devices with their start and end apart: 8, of which 8 were waited for; matrix products, arithmetic and copies ran while one was open for 0% of the time, Pallas kernels for 0%

commit v1 on v0

v1 whole, which is shorter than its diff:
```python
import functools

import jax
import jax.numpy as jnp
from jax import lax
from jax.experimental import pallas as pl
from jax.experimental.pallas import tpu as pltpu
from jax.sharding import PartitionSpec as P

F32 = jnp.float32
BF16 = jnp.bfloat16
VMEM_SPEC = pl.BlockSpec(memory_space=pltpu.VMEM)
SMEM_SPEC = pl.BlockSpec(memory_space=pltpu.SMEM)


def from_behind(value, axis, steps):
    count = lax.axis_size(axis)
    pairs = [(source, (source + steps) % count) for source in range(count)]
    return lax.ppermute(value, axis, pairs)


def member_parts(value):
    if lax.axis_size("mem") == 2:
        return [value, from_behind(value, "mem", 1)]
    return [lax.psum(value, "mem")]


def halves(value):
    high = value.astype(BF16)
    return high, (value - high.astype(F32)).astype(BF16)


def mm(a, b):
    return jnp.dot(a, b, preferred_element_type=F32)


def mm3(a, b):
    a_high, a_low = halves(a)
    b_high, b_low = halves(b)
    return mm(a_high, b_high) + (mm(a_high, b_low) + mm(a_low, b_high))


def mm_full(a, b):
    return jnp.dot(a, b, precision=lax.Precision.HIGHEST, preferred_element_type=F32)


def nt(a, b):
    return lax.dot_general(a, b, (((1,), (1,)), ((), ())), preferred_element_type=F32)


def weigh_kernel(scale, part_count, *refs):
    parts = refs[:part_count]
    d_ref, w_ref, inv = refs[part_count:]
    total = parts[0][...]
    for part in parts[1:]:
        total = total + part[...]
    size = total.shape[0]
    eye = (
        lax.broadcasted_iota(jnp.int32, (size, size), 0)
        == lax.broadcasted_iota(jnp.int32, (size, size), 1)
    ).astype(F32)
    spd = total * scale + eye
    square = mm3(spd, spd)
    bound2 = jnp.max(jnp.sum(jnp.abs(square), axis=1))
    row = jnp.max(jnp.sum(jnp.abs(spd), axis=1))
    top = jnp.minimum(row, jnp.sqrt(bound2 * 1.01)) * 1.001
    ratio = (top - 1.0) / (top + 1.0)
    alpha = 2.0 / (top + 1.0)
    gain = 2.0 / (2.0 - ratio * ratio)
    c0 = 2.0 * alpha * gain
    c1 = -alpha * alpha * gain
    ratio = ratio * ratio * 0.5 * gain
    inv[...] = c0 * eye + c1 * spd
    small = top < 40.0

    def run(product, active):
        def going(ratio):
            return jnp.logical_and(active, ratio > 2e-5)

        def step(ratio):
            now = inv[...]
            gain = 2.0 / (2.0 - ratio * ratio)
            inv[...] = gain * (2.0 * now - product(now, product(spd, now)))
            return ratio * ratio * 0.5 * gain

        lax.while_loop(going, step, ratio)

    run(mm3, small)
    run(mm_full, jnp.logical_not(small))

    @pl.when(small)
    def _():
        w_ref[...] = mm3(inv[...], d_ref[...]).astype(BF16)

    @pl.when(jnp.logical_not(small))
    def _():
        now = inv[...]
        first = mm_full(now, d_ref[...])
        left = d_ref[...] - mm_full(spd, first)
        w_ref[...] = (first + mm_full(now, left)).astype(BF16)


def link_kernel(count, order_ref, *refs):
    ys = refs[:count]
    ws = refs[count : 2 * count]
    g_ref, sorted_ref, y_sorted = refs[2 * count :]
    for step in range(count):
        for offset in range(count):

            @pl.when(order_ref[0, step] == offset)
            def _():
                y_sorted[step] = ys[offset][...]
                sorted_ref[step] = ws[offset][...]

    place = 0
    for step in range(1, count):
        for before in range(step):
            g_ref[place] = nt(sorted_ref[before], y_sorted[step])
            place += 1


def apply_kernel(scale, count, part_count, *refs):
    order_ref, pattern_ref, distance_ref, taper_ref = refs[:4]
    refs = refs[4:]
    crosses = [refs[part_count * a : part_count * (a + 1)] for a in range(count)]
    refs = refs[part_count * count :]
    links = refs[:part_count]
    w_ref, x_ref, out_ref, cross_now = refs[part_count:]
    block = pl.program_id(0)
    cols = cross_now.shape[1]
    q_count = pattern_ref.shape[3]
    lane = lax.broadcasted_iota(jnp.int32, (1, cols), 1)
    applied = []
    field = x_ref[...]
    place = 0
    for step in range(count):
        offset = order_ref[0, step]
        for a in range(count):

            @pl.when(offset == a)
            def _():
                total = crosses[a][0][...]
                for part in crosses[a][1:]:
                    total = total + part[...]
                cross_now[...] = total

        weight = jnp.zeros((1, cols), F32)
        for q in range(q_count):
            value = pattern_ref[0, offset, block, q].astype(F32) * taper_ref[
                distance_ref[0, offset, block, q]
            ]
            inside = (lane >= q * (cols // q_count)) & (lane < (q + 1) * (cols // q_count))
            weight = jnp.where(inside, value, weight)
        cross = cross_now[...]
        for before in range(step):
            link = links[0][place]
            for part in links[1:]:
                link = link + part[place]
            place += 1
            link_high, link_low = halves(link)
            high, low = applied[before]
            cross = cross + (mm(high, link_high) + (mm(high, link_low) + mm(low, link_high)))
        applied.append(halves(cross * scale * weight))
        high, low = applied[-1]
        field = field + (mm(high, w_ref[step]) + mm(low, w_ref[step]))
    out_ref[...] = field


def on_device(state, obs_anom, innov, pattern, distance, taper, order):
    cells, own_members = state.shape
    members = lax.axis_size("mem") * own_members
    scale = 1.0 / (members - 1)
    num_obs = obs_anom.shape[0]
    arrivals = order.shape[1]
    row_blocks = pattern.shape[2]
    rows = cells // row_blocks
    gram_parts = member_parts(nt(obs_anom, obs_anom))
    ys = [obs_anom] + [from_behind(obs_anom, "band", a) for a in range(1, arrivals)]
    weights = pl.pallas_call(
        functools.partial(weigh_kernel, scale, len(gram_parts)),
        out_shape=jax.ShapeDtypeStruct(innov.shape, BF16),
        in_specs=[VMEM_SPEC] * (len(gram_parts) + 1),
        out_specs=VMEM_SPEC,
        scratch_shapes=[pltpu.VMEM((num_obs, num_obs), F32)],
        cost_estimate=pl.CostEstimate(
            flops=60 * num_obs**3, bytes_accessed=8 * innov.size, transcendentals=0
        ),
    )(*gram_parts, innov)
    ws = [weights] + [from_behind(weights, "band", a) for a in range(1, arrivals)]
    state_high = state.astype(BF16)
    crosses = [member_parts(nt(state_high, y)) for y in ys]
    pairs = arrivals * (arrivals - 1) // 2
    link, w_sorted = pl.pallas_call(
        functools.partial(link_kernel, arrivals),
        out_shape=(
            jax.ShapeDtypeStruct((pairs, num_obs, num_obs), F32),
            jax.ShapeDtypeStruct((arrivals,) + obs_anom.shape, BF16),
        ),
        in_specs=[SMEM_SPEC] + [VMEM_SPEC] * (2 * arrivals),
        out_specs=(VMEM_SPEC, VMEM_SPEC),
        scratch_shapes=[pltpu.VMEM((arrivals,) + obs_anom.shape, BF16)],
    )(order, *ys, *ws)
    links = member_parts(link)
    part_count = len(links)
    row_spec = pl.BlockSpec((rows, num_obs), lambda i: (i, 0))
    field_spec = pl.BlockSpec((rows, own_members), lambda i: (i, 0))
    return pl.pallas_call(
        functools.partial(apply_kernel, scale, arrivals, part_count),
        out_shape=jax.ShapeDtypeStruct(state.shape, F32),
        grid=(row_blocks,),
        in_specs=[SMEM_SPEC] * 4
        + [row_spec] * (arrivals * part_count)
        + [pl.BlockSpec((pairs, num_obs, num_obs), lambda i: (0, 0, 0))] * part_count
        + [pl.BlockSpec((arrivals,) + obs_anom.shape, lambda i: (0, 0, 0)), field_spec],
        out_specs=field_spec,
        scratch_shapes=[pltpu.VMEM((rows, num_obs), F32)],
    )(
        order,
        pattern,
        distance,
        taper,
        *[part for cross in crosses for part in cross],
        *links,
        w_sorted,
        state,
    )


def solution(mesh):
    return jax.shard_map(
        on_device,
        mesh=mesh,
        in_specs=(
            P("band", "mem"),
            P("band", "mem"),
            P("band", "mem"),
            P("band", None, None, None),
            P("band", None, None, None),
            P(),
            P("band", None),
        ),
        out_specs=P("band", "mem"),
        check_vma=False,
    )
```

time: 314 us -> 117 us (0.37)
  waiting for transfers between devices: 173 us -> 39.5 us
  other arithmetic: 58 us -> 2.51 us
  matrix products: 43.7 us -> 10.6 us
  Pallas kernels: 0 us -> 31.9 us
  starting transfers between devices: 2.48 us -> 29.2 us
  between operations: 22.5 us -> 0.28 us
  local copies, waits for them, and re-layouts: 13.5 us -> 2.44 us
    psum x5 -> x0, waiting for transfers between devices: 92.7 us -> none  [the longest x4 71 us: on_device(): cross = lax.psum(cross_part, 'mem')]
    another operation x12 -> x0, other arithmetic: 55.9 us -> none  [the longest x6 34 us: on_device(): factor = jnp.linalg.cholesky(spd)]
    ppermute x3 -> x12, waiting for transfers between devices: 80.5 us -> 39.5 us  [from_behind(): return lax.ppermute(value, axis, pairs)]
    pallas_call x0 -> x3, Pallas kernels: none -> 31.9 us  [the longest x1 20.8 us: on_device(): pl.pallas_call(functools.partial(apply_kernel, scale, arrivals, part_coun...]
    dot_general x9 -> x5, matrix products: 39.6 us -> 10.6 us  [nt(): lax.dot_general(a, b, (((1,), (1,)), ((), ())), preferred_element_type=F32)]
    ppermute x3 -> x12, starting transfers between devices: 1.83 us -> 29.2 us  [from_behind(): return lax.ppermute(value, axis, pairs)]
    unnamed x22 -> x16, local copies, waits for them, and re-layouts: 7.98 us -> 2.44 us
    another operation x9 -> x0, local copies, waits for them, and re-layouts: 4.12 us -> none
  transfers between devices with their start and end apart: 8 -> 12, of which waited for: 8 -> 3; matrix products, arithmetic and copies ran while one was open for 0% -> 12% of each run, Pallas kernels for 0% -> 9%
where the time goes in v1:
time: 117 us; the launch traced here: 116 us
  waiting for transfers between devices  39.5 us (34%)
  Pallas kernels  31.9 us (27%)
  starting transfers between devices  29.2 us (25%)
  matrix products  10.6 us (9%)
  other arithmetic  2.51 us (2%)
  local copies, waits for them, and re-layouts  2.44 us (2%)
    ppermute x12, waiting for transfers between devices, from_behind(): return lax.ppermute(value, axis, pairs)  39.5 us
    ppermute x12, starting transfers between devices, from_behind(): return lax.ppermute(value, axis, pairs)  29.2 us
    pallas_call x1, Pallas kernels, on_device(): pl.pallas_call(functools.partial(apply_kernel, scale, arrivals, part_coun...  20.8 us
    dot_general x5, matrix products, nt(): lax.dot_general(a, b, (((1,), (1,)), ((), ())), preferred_element_type=F32)  10.6 us
    pallas_call x1, Pallas kernels, on_device(): pl.pallas_call(functools.partial(weigh_kernel, scale, len(gram_parts)), o...  6.21 us
    pallas_call x1, Pallas kernels, on_device(): pl.pallas_call(functools.partial(link_kernel, arrivals), out_shape=(jax.S...  4.85 us
    convert_element_type x1, other arithmetic, on_device(): state_high = state.astype(BF16)  2.51 us
    unnamed x16, local copies, waits for them, and re-layouts  2.44 us
  transfers between devices with their start and end apart: 12, of which 3 were waited for; matrix products, arithmetic and copies ran while one was open for 12% of the time, Pallas kernels for 9%

profile of v1, /device:TPU:0, one launch (start us, length us, event | category | flops | bytes accessed | tf_op | source)
XLA Modules:
  0.0 116.5 jit_solution(13765955261749070043)
XLA Ops:
  0.0 3.0 %collective-permute-start.1 = (bf16[256,1024]{1,0:T(8,128)(2,1)}, bf16[256,1024]{1,0:T(8,128)(2,1)S(1)}, u32[]{:S(2)}, u32[]{:S(2)}) collective-permute-start(bf16[256,1024]{1,0:T(8,128)(2,1)} %refs_0_.2), channel_id=1, source_target_pairs={{0,2},{2,4},{4,6},{6,8},{8,10},{10,12},{12,14},{14,16},{16,18},{18... | collective-permute-start | bytes 1572872 | tf_op jit(solution)/shard_map/ppermute | solution.py:19
  3.0 1.5 %fusion.4.refs_0_ = f32[256,256]{1,0:T(8,128)S(1)} fusion(bf16[256,1024]{1,0:T(8,128)(2,1)} %refs_0_.2), kind=kOutput, calls=%fused_computation.4 | convolution fusion | flops 134217728 | bytes 786432 | tf_op jit(solution)/shard_map/dot_general | solution.py:48
  4.5 0.0 copy-start.4
  4.5 0.1 collective-permute-start.7
  4.6 2.5 %collective-permute-start.5 = (bf16[256,1024]{1,0:T(8,128)(2,1)}, bf16[256,1024]{1,0:T(8,128)(2,1)}, u32[]{:S(2)}, u32[]{:S(2)}) collective-permute-start(bf16[256,1024]{1,0:T(8,128)(2,1)} %refs_0_.2), channel_id=1, source_target_pairs={{0,6},{2,8},{4,10},{6,12},{8,14},{10,16},{12,18},{14,20},{16,22},{... | collective-permute-start | bytes 1572872 | tf_op jit(solution)/shard_map/ppermute | solution.py:19
  7.1 1.5 %collective-permute-start.3 = (bf16[256,1024]{1,0:T(8,128)(2,1)}, bf16[256,1024]{1,0:T(8,128)(2,1)}, u32[]{:S(2)}, u32[]{:S(2)}) collective-permute-start(bf16[256,1024]{1,0:T(8,128)(2,1)} %refs_0_.2), channel_id=1, source_target_pairs={{0,4},{2,6},{4,8},{6,10},{8,12},{10,14},{12,16},{14,18},{16,20},{1... | collective-permute-start | bytes 1572872 | tf_op jit(solution)/shard_map/ppermute | solution.py:19
  8.6 2.5 %convert_element_type.3 = bf16[1024,1024]{1,0:T(8,128)(2,1)S(1)} convert(f32[1024,1024]{1,0:T(8,128)} %refs_15_.1) | non-fusion elementwise | flops 1048576 | bytes 6291456 | tf_op jit(solution)/shard_map/convert_element_type | solution.py:190
  11.1 0.0 copy-done.4
  11.1 0.0 copy-start
  11.2 0.0 collective-permute-done.7.refs_1_
  11.2 6.2 %shard_map.73.refs_4_ = bf16[256,1024]{1,0:T(8,128)(2,1)} custom-call(f32[256,256]{1,0:T(8,128)} %copy-done.4, f32[256,256]{1,0:T(8,128)} %collective-permute-done.7.refs_1_, f32[256,1024]{1,0:T(8,128)} %refs_2_.2), custom_call_target="tpu_custom_call" | custom-call | flops 1006632960 | bytes 2097152 | tf_op jit(solution)/shard_map/pallas_call | solution.py:179
  17.4 1.6 %collective-permute-start.10 = (bf16[256,1024]{1,0:T(8,128)(2,1)}, bf16[256,1024]{1,0:T(8,128)(2,1)}, u32[]{:S(2)}, u32[]{:S(2)}) collective-permute-start(bf16[256,1024]{1,0:T(8,128)(2,1)} %shard_map.73.refs_4_), channel_id=1, source_target_pairs={{0,6},{2,8},{4,10},{6,12},{8,14},{10,16},{12,18},{14,20},{16,22},{... | collective-permute-start | bytes 1572872 | tf_op jit(solution)/shard_map/ppermute | solution.py:19
  18.9 1.5 %collective-permute-start.9 = (bf16[256,1024]{1,0:T(8,128)(2,1)}, bf16[256,1024]{1,0:T(8,128)(2,1)}, u32[]{:S(2)}, u32[]{:S(2)}) collective-permute-start(bf16[256,1024]{1,0:T(8,128)(2,1)} %shard_map.73.refs_4_), channel_id=1, source_target_pairs={{0,4},{2,6},{4,8},{6,10},{8,12},{10,14},{12,16},{14,18},{16,20},{1... | collective-permute-start | bytes 1572872 | tf_op jit(solution)/shard_map/ppermute | solution.py:19
  20.5 0.0 collective-permute-done.1.refs_1_
  20.5 0.0 copy-start.3
  20.5 18.0 %collective-permute-start.8 = (bf16[256,1024]{1,0:T(8,128)(2,1)}, bf16[256,1024]{1,0:T(8,128)(2,1)}, u32[]{:S(2)}, u32[]{:S(2)}) collective-permute-start(bf16[256,1024]{1,0:T(8,128)(2,1)} %shard_map.73.refs_4_), channel_id=1, source_target_pairs={{0,2},{2,4},{4,6},{6,8},{8,10},{10,12},{12,14},{14,16},{16,18},{18... | collective-permute-start | bytes 1572872 | tf_op jit(solution)/shard_map/ppermute | solution.py:19
  38.4 0.0 copy-done.3
  38.4 0.0 copy-done
  38.4 1.8 %fusion.refs_4_ = f32[1024,256]{1,0:T(8,128)} fusion(bf16[1024,1024]{1,0:T(8,128)(2,1)S(1)} %convert_element_type.3, bf16[256,1024]{1,0:T(8,128)(2,1)S(1)} %copy-done), kind=kOutput, calls=%fused_computation | convolution fusion | flops 536870912 | bytes 3670016 | tf_op jit(solution)/shard_map/dot_general | solution.py:48
  40.2 1.8 %fusion.1.refs_6_ = f32[1024,256]{1,0:T(8,128)S(1)} fusion(bf16[1024,1024]{1,0:T(8,128)(2,1)S(1)} %convert_element_type.3, bf16[256,1024]{1,0:T(8,128)(2,1)} %copy-done.3), kind=kOutput, calls=%fused_computation.1 | convolution fusion | flops 536870912 | bytes 3670016 | tf_op jit(solution)/shard_map/dot_general | solution.py:48
  42.0 0.0 copy-start.1
  42.0 0.0 collective-permute-done.5.refs_3_
  42.0 0.1 collective-permute-start
  42.1 0.0 collective-permute-done.3.refs_2_
  42.1 0.5 collective-permute-start.2
  42.6 0.0 collective-permute-done.10.refs_7_
  42.6 20.5 %collective-permute-done.9.refs_6_ = bf16[256,1024]{1,0:T(8,128)(2,1)} collective-permute-done((bf16[256,1024]{1,0:T(8,128)(2,1)}, bf16[256,1024]{1,0:T(8,128)(2,1)}, u32[]{:S(2)}, u32[]{:S(2)}) %collective-permute-start.9) | collective-permute-done | bytes 524320 | tf_op jit(solution)/shard_map/ppermute | solution.py:19
  63.1 17.5 %collective-permute-done.8.refs_5_ = bf16[256,1024]{1,0:T(8,128)(2,1)} collective-permute-done((bf16[256,1024]{1,0:T(8,128)(2,1)}, bf16[256,1024]{1,0:T(8,128)(2,1)}, u32[]{:S(2)}, u32[]{:S(2)}) %collective-permute-start.8) | collective-permute-done | bytes 524320 | tf_op jit(solution)/shard_map/ppermute | solution.py:19
  80.7 4.8 %shard_map.74 = (f32[6,256,256]{2,1,0:T(8,128)}, bf16[4,256,1024]{2,1,0:T(8,128)(2,1)}) custom-call(s32[1,4]{1,0:T(1,128)} %refs_0_.3, bf16[256,1024]{1,0:T(8,128)(2,1)} %refs_0_.2, bf16[256,1024]{1,0:T(8,128)(2,1)} %copy-done.3, bf16[256,1024]{1,0:T(8,128)(2,1)} %collective-permute-done.3.refs_2_, bf16[256,1024]{1,0:T(8,128)(2,1)} %collective-permute-done.5.refs_3_, ...), custom_call_target="tpu_custom_call" | custom-call | tf_op jit(solution)/shard_map/pallas_call | solution.py:193
  85.5 0.0 copy-done.1
  85.5 0.0 collective-permute-start.11
  85.5 2.8 %fusion.2.refs_8_ = f32[1024,256]{1,0:T(8,128)} fusion(bf16[1024,1024]{1,0:T(8,128)(2,1)S(1)} %convert_element_type.3, bf16[256,1024]{1,0:T(8,128)(2,1)} %collective-permute-done.3.refs_2_), kind=kOutput, calls=%fused_computation.2 | convolution fusion | flops 536870912 | bytes 3670016 | tf_op jit(solution)/shard_map/dot_general | solution.py:48
  88.3 0.0 copy-start.5
  88.3 0.0 copy-start.6
  88.3 0.5 collective-permute-start.4
  88.8 2.8 %fusion.3.refs_10_ = f32[1024,256]{1,0:T(8,128)} fusion(bf16[1024,1024]{1,0:T(8,128)(2,1)S(1)} %convert_element_type.3, bf16[256,1024]{1,0:T(8,128)(2,1)} %collective-permute-done.5.refs_3_), kind=kOutput, calls=%fused_computation.3 | convolution fusion | flops 536870912 | bytes 3670016 | tf_op jit(solution)/shard_map/dot_general | solution.py:48
  91.6 0.0 collective-permute-start.6
  91.6 0.0 copy-done.5
  91.6 0.7 copy.8.refs_1_
  92.3 0.0 copy-done.6
  92.3 0.7 copy.9.refs_2_
  93.0 0.0 collective-permute-done.refs_5_
  93.0 0.0 collective-permute-done.2.refs_7_
  93.0 0.0 collective-permute-done.4.refs_9_
  93.0 1.4 %collective-permute-done.6.refs_11_ = f32[1024,256]{1,0:T(8,128)S(1)} collective-permute-done((f32[1024,256]{1,0:T(8,128)}, f32[1024,256]{1,0:T(8,128)S(1)}, u32[]{:S(2)}, u32[]{:S(2)}) %collective-permute-start.6) | collective-permute-done | bytes 1048608 | tf_op jit(solution)/shard_map/ppermute | solution.py:19
  94.5 0.0 copy-start.2
  94.5 0.0 collective-permute-done.11.refs_13_
  94.5 1.0 copy-done.2
  95.5 20.8 %shard_map.75 = f32[1024,1024]{1,0:T(8,128)} custom-call(s32[1,4]{1,0:T(1,128)} %refs_0_.3, s32[1,4,8,4]{3,2,1,0:T(8,128)} %copy.8.refs_1_, s32[1,4,8,4]{3,2,1,0:T(8,128)} %copy.9.refs_2_, f32[8]{0:T(128)} %refs_3_.1, f32[1024,256]{1,0:T(8,128)} %fusion.refs_4_, f32[1024,256]{1,0:T(8,128)} %collective-permute-done.refs_5_, f32[1024,256]{1,0:T(8,128)} %copy-done.1, ...), custom_call_target="tpu_custom_call" | custom-call | tf_op jit(solution)/shard_map/pallas_call | solution.py:207
Async XLA Ops:
  0.0 20.5 %collective-permute-start.1 = (bf16[256,1024]{1,0:T(8,128)(2,1)}, bf16[256,1024]{1,0:T(8,128)(2,1)S(1)}, u32[]{:S(2)}, u32[]{:S(2)}) collective-permute-start(bf16[256,1024]{1,0:T(8,128)(2,1)} %refs_0_.2), channel_id=1, source_target_pairs={{0,2},{2,4},{4,6},{6,8},{8,10},{10,12},{12,14},{14,16},{16,18},{18... | collective-permute-start | bytes 1572872 | tf_op jit(solution)/shard_map/ppermute | solution.py:19
  4.5 6.6 %copy-start.4 = (f32[256,256]{1,0:T(8,128)}, f32[256,256]{1,0:T(8,128)S(1)}, u32[]{:S(2)}) copy-start(f32[256,256]{1,0:T(8,128)S(1)} %fusion.4.refs_0_) | copy-start | bytes 786436
  4.5 6.6 %collective-permute-start.7 = (f32[256,256]{1,0:T(8,128)S(1)}, f32[256,256]{1,0:T(8,128)}, u32[]{:S(2)}, u32[]{:S(2)}) collective-permute-start(f32[256,256]{1,0:T(8,128)S(1)} %fusion.4.refs_0_), channel_id=1, source_target_pairs={{0,1},{1,0},{2,3},{3,2},{4,5},{5,4},{6,7},{7,6},{8,9},{9,8},{10,11... | collective-permute-start | bytes 786440 | tf_op jit(solution)/shard_map/ppermute | solution.py:19
  4.6 37.4 %collective-permute-start.5 = (bf16[256,1024]{1,0:T(8,128)(2,1)}, bf16[256,1024]{1,0:T(8,128)(2,1)}, u32[]{:S(2)}, u32[]{:S(2)}) collective-permute-start(bf16[256,1024]{1,0:T(8,128)(2,1)} %refs_0_.2), channel_id=1, source_target_pairs={{0,6},{2,8},{4,10},{6,12},{8,14},{10,16},{12,18},{14,20},{16,22},{... | collective-permute-start | bytes 1572872 | tf_op jit(solution)/shard_map/ppermute | solution.py:19
  7.1 35.0 %collective-permute-start.3 = (bf16[256,1024]{1,0:T(8,128)(2,1)}, bf16[256,1024]{1,0:T(8,128)(2,1)}, u32[]{:S(2)}, u32[]{:S(2)}) collective-permute-start(bf16[256,1024]{1,0:T(8,128)(2,1)} %refs_0_.2), channel_id=1, source_target_pairs={{0,4},{2,6},{4,8},{6,10},{8,12},{10,14},{12,16},{14,18},{16,20},{1... | collective-permute-start | bytes 1572872 | tf_op jit(solution)/shard_map/ppermute | solution.py:19
  11.1 27.3 %copy-start = (bf16[256,1024]{1,0:T(8,128)(2,1)S(1)}, bf16[256,1024]{1,0:T(8,128)(2,1)}, u32[]{:S(2)}) copy-start(bf16[256,1024]{1,0:T(8,128)(2,1)} %refs_0_.2) | copy-start | bytes 1572868
  17.4 25.2 %collective-permute-start.10 = (bf16[256,1024]{1,0:T(8,128)(2,1)}, bf16[256,1024]{1,0:T(8,128)(2,1)}, u32[]{:S(2)}, u32[]{:S(2)}) collective-permute-start(bf16[256,1024]{1,0:T(8,128)(2,1)} %shard_map.73.refs_4_), channel_id=1, source_target_pairs={{0,6},{2,8},{4,10},{6,12},{8,14},{10,16},{12,18},{14,20},{16,22},{... | collective-permute-start | bytes 1572872 | tf_op jit(solution)/shard_map/ppermute | solution.py:19
  18.9 44.2 %collective-permute-start.9 = (bf16[256,1024]{1,0:T(8,128)(2,1)}, bf16[256,1024]{1,0:T(8,128)(2,1)}, u32[]{:S(2)}, u32[]{:S(2)}) collective-permute-start(bf16[256,1024]{1,0:T(8,128)(2,1)} %shard_map.73.refs_4_), channel_id=1, source_target_pairs={{0,4},{2,6},{4,8},{6,10},{8,12},{10,14},{12,16},{14,18},{16,20},{1... | collective-permute-start | bytes 1572872 | tf_op jit(solution)/shard_map/ppermute | solution.py:19
  20.5 18.0 %copy-start.3 = (bf16[256,1024]{1,0:T(8,128)(2,1)}, bf16[256,1024]{1,0:T(8,128)(2,1)S(1)}, u32[]{:S(2)}) copy-start(bf16[256,1024]{1,0:T(8,128)(2,1)S(1)} %collective-permute-done.1.refs_1_) | copy-start | bytes 1572868
  20.5 60.2 %collective-permute-start.8 = (bf16[256,1024]{1,0:T(8,128)(2,1)}, bf16[256,1024]{1,0:T(8,128)(2,1)}, u32[]{:S(2)}, u32[]{:S(2)}) collective-permute-start(bf16[256,1024]{1,0:T(8,128)(2,1)} %shard_map.73.refs_4_), channel_id=1, source_target_pairs={{0,2},{2,4},{4,6},{6,8},{8,10},{10,12},{12,14},{14,16},{16,18},{18... | collective-permute-start | bytes 1572872 | tf_op jit(solution)/shard_map/ppermute | solution.py:19
  42.0 43.5 %copy-start.1 = (f32[1024,256]{1,0:T(8,128)}, f32[1024,256]{1,0:T(8,128)S(1)}, u32[]{:S(2)}) copy-start(f32[1024,256]{1,0:T(8,128)S(1)} %fusion.1.refs_6_) | copy-start | bytes 3145732
  42.0 51.0 %collective-permute-start = (f32[1024,256]{1,0:T(8,128)}, f32[1024,256]{1,0:T(8,128)}, u32[]{:S(2)}, u32[]{:S(2)}) collective-permute-start(f32[1024,256]{1,0:T(8,128)} %fusion.refs_4_), channel_id=1, source_target_pairs={{0,1},{1,0},{2,3},{3,2},{4,5},{5,4},{6,7},{7,6},{8,9},{9,8},{10,11... | collective-permute-start | bytes 3145736 | tf_op jit(solution)/shard_map/ppermute | solution.py:19
  42.1 50.9 %collective-permute-start.2 = (f32[1024,256]{1,0:T(8,128)S(1)}, f32[1024,256]{1,0:T(8,128)}, u32[]{:S(2)}, u32[]{:S(2)}) collective-permute-start(f32[1024,256]{1,0:T(8,128)S(1)} %fusion.1.refs_6_), channel_id=1, source_target_pairs={{0,1},{1,0},{2,3},{3,2},{4,5},{5,4},{6,7},{7,6},{8,9},{9,8},{10,11... | collective-permute-start | bytes 3145736 | tf_op jit(solution)/shard_map/ppermute | solution.py:19
  85.5 9.0 %collective-permute-start.11 = (f32[6,256,256]{2,1,0:T(8,128)}, f32[6,256,256]{2,1,0:T(8,128)}, u32[]{:S(2)}, u32[]{:S(2)}) collective-permute-start(f32[6,256,256]{2,1,0:T(8,128)} %get-tuple-element.7.refs_12_), channel_id=1, source_target_pairs={{0,1},{1,0},{2,3},{3,2},{4,5},{5,4},{6,7},{7,6},{8,9},{9,8},{10,11... | collective-permute-start | bytes 4718600 | tf_op jit(solution)/shard_map/ppermute | solution.py:19
  88.3 3.3 %copy-start.5 = (s32[1,4,8,4]{2,3,1,0:T(4,128)S(1)}, s32[1,4,8,4]{2,3,1,0:T(4,128)}, u32[]{:S(2)}) copy-start(s32[1,4,8,4]{2,3,1,0:T(4,128)} %param.10) | copy-start | bytes 1540
  88.3 4.0 %copy-start.6 = (s32[1,4,8,4]{2,3,1,0:T(4,128)S(1)}, s32[1,4,8,4]{2,3,1,0:T(4,128)}, u32[]{:S(2)}) copy-start(s32[1,4,8,4]{2,3,1,0:T(4,128)} %param.11) | copy-start | bytes 1540
  88.3 4.7 %collective-permute-start.4 = (f32[1024,256]{1,0:T(8,128)}, f32[1024,256]{1,0:T(8,128)}, u32[]{:S(2)}, u32[]{:S(2)}) collective-permute-start(f32[1024,256]{1,0:T(8,128)} %fusion.2.refs_8_), channel_id=1, source_target_pairs={{0,1},{1,0},{2,3},{3,2},{4,5},{5,4},{6,7},{7,6},{8,9},{9,8},{10,11... | collective-permute-start | bytes 3145736 | tf_op jit(solution)/shard_map/ppermute | solution.py:19
  91.6 2.9 %collective-permute-start.6 = (f32[1024,256]{1,0:T(8,128)}, f32[1024,256]{1,0:T(8,128)S(1)}, u32[]{:S(2)}, u32[]{:S(2)}) collective-permute-start(f32[1024,256]{1,0:T(8,128)} %fusion.3.refs_10_), channel_id=1, source_target_pairs={{0,1},{1,0},{2,3},{3,2},{4,5},{5,4},{6,7},{7,6},{8,9},{9,8},{10,11... | collective-permute-start | bytes 3145736 | tf_op jit(solution)/shard_map/ppermute | solution.py:19
  94.5 1.0 copy-start.2
